TPU v7x, 512 devices: a whole 4x4x16 slice. The times are simulated.
512 devices in a mesh: blk: 32 (over z_lo, y), seq: 16 (over z_hi, x, core).
Axes of the slice: x: 4, y: 4, z: 16 (z_hi: 2, z_lo: 8; z = z_hi * 8 + z_lo), core: 2. Of those that a mesh axis runs over, the one named last changes fastest.
Arguments:
- tokens: bfloat16 [12288, 4096], P('seq', 'blk'), may hold values from -6 to 6
- grad_out: bfloat16 [12288, 4096], P('seq', 'blk'), may hold values from -0.0546875 to 0.0546875
- input_weight_blocks: bfloat16 [1024, 128, 128], P('blk'), may hold values from -0.25 to 0.25
- output_weight_blocks: bfloat16 [1024, 128, 128], P('blk'), may hold values from -0.25 to 0.25
- row_ids: int32 [1024], P('blk'), may hold values from 0 to 31, as said below
- lengths: int32 [16], P('seq'), may hold values from 1 to 768, 7680 in all
Outputs:
- grad_in: bfloat16 [1024, 128, 128], P('blk', 'seq')
- grad_w_out: bfloat16 [1024, 128, 128], P('blk', 'seq')
Inputs may be any that keep to these rules, and one draw needn't show every extreme that they name: `row_ids`: the 4 blocks of each hidden column block have distinct row blocks. `lengths`: some window is full.
All inputs are finite; a program needn't handle non-finite values. No bound on the sum of `lengths` on one device may be relied on, other than what follows from the above.
Results may differ from a plain program's by a relative error of at most 0.015.
Values may be sent and summed in bfloat16 or wider, within the bound.
No kernel may reach another device: no remote copies, remote signals or barrier semaphores. Data moves between devices by JAX's collectives and lax.ppermute only.
A program may use at most 64 MiB of HBM per device.

v0:
```python
import jax
import jax.numpy as jnp
from jax import lax
from jax.sharding import PartitionSpec as P

BLOCK_SIDE = 128
BLOCKS_PER_COLUMN = 4
gelu_scale = 0.7978845608


def gelu_pair(pre_act):
    tanh_val = jnp.tanh(gelu_scale * (pre_act + 0.044715 * pre_act * pre_act * pre_act))
    activation = 0.5 * pre_act * (1.0 + tanh_val)
    gelu_slope = 0.5 * (1.0 + tanh_val) + 0.5 * pre_act * (
        1.0 - tanh_val * tanh_val
    ) * gelu_scale * (1.0 + 0.134145 * pre_act * pre_act)
    return (activation, gelu_slope)


def shards(tokens, grad_out, input_weight_blocks, output_weight_blocks, row_ids, lengths):
    tok_rows = tokens.shape[0]
    groups = input_weight_blocks.shape[0] // BLOCKS_PER_COLUMN
    live_rows = lax.iota(jnp.int32, tok_rows)[:, None] < lengths[0]
    masked = jnp.where(live_rows, grad_out, jnp.zeros_like(grad_out))
    features = lax.all_gather(tokens, "blk", axis=1, tiled=True)
    x_slots = features.reshape(tok_rows, -1, BLOCK_SIDE)[:, row_ids, :]
    pre_slot = jnp.einsum(
        "tkc,kch->tkh", x_slots, input_weight_blocks, preferred_element_type=jnp.float32
    )
    pre_act = pre_slot.reshape(tok_rows, groups, BLOCKS_PER_COLUMN, BLOCK_SIDE).sum(2)
    activation, gelu_slope = gelu_pair(pre_act)
    activation = activation.astype(jnp.bfloat16)
    gradient = lax.all_gather(masked, "blk", axis=1, tiled=True)
    gradient_slots = gradient.reshape(tok_rows, -1, BLOCK_SIDE)[:, row_ids, :]
    g_four = gradient_slots.reshape(tok_rows, groups, BLOCKS_PER_COLUMN, BLOCK_SIDE)
    output_share = jnp.einsum(
        "tgh,tgrf->grhf", activation, g_four, preferred_element_type=jnp.float32
    )
    output_share = output_share.reshape(-1, BLOCK_SIDE, BLOCK_SIDE)
    slot_gradient = jnp.einsum(
        "xcn,cpn->xcp", gradient_slots, output_weight_blocks, preferred_element_type=jnp.float32
    )
    grad_act = slot_gradient.reshape(tok_rows, groups, BLOCKS_PER_COLUMN, BLOCK_SIDE).sum(2)
    grad_pre = (grad_act * gelu_slope).astype(jnp.bfloat16)
    x_four = x_slots.reshape(tok_rows, groups, BLOCKS_PER_COLUMN, BLOCK_SIDE)
    input_share = jnp.einsum("tgrc,tgh->grch", x_four, grad_pre, preferred_element_type=jnp.float32)
    input_share = input_share.reshape(-1, BLOCK_SIDE, BLOCK_SIDE)
    in_total, out_total = (
        lax.psum_scatter(
            input_share.astype(jnp.bfloat16), "seq", scatter_dimension=1, tiled=True
        ).astype(jnp.float32),
        lax.psum_scatter(
            output_share.astype(jnp.bfloat16), "seq", scatter_dimension=1, tiled=True
        ).astype(jnp.float32),
    )
    return (in_total.astype(jnp.bfloat16), out_total.astype(jnp.bfloat16))


def solution(mesh):
    return jax.shard_map(
        shards,
        mesh=mesh,
        in_specs=(
            P("seq", "blk"),
            P("seq", "blk"),
            P("blk", None, None),
            P("blk", None, None),
            P("blk"),
            P("seq"),
        ),
        out_specs=(P("blk", "seq", None), P("blk", "seq", None)),
        check_vma=False,
    )
```

profile of v0, /device:TPU:8, one launch (start us, length us, event | category | flops | bytes accessed | tf_op | source)
XLA Modules:
  0.0 731.5 jit_solution(1183288286320728725)
XLA Ops:
  7.2 0.0 copy-start
  7.2 0.0 all-gather.3.cloned.1.call-start
  7.2 1.8 copy.21
  9.1 0.0 all-gather.3.cloned.1.call-update
  9.1 0.0 all-gather.5.cloned.1.call-start
  9.8 1.1 copy.23
  10.9 0.7 broadcast_select_fusion
  11.6 0.0 all-gather.5.cloned.1.call-update
  11.6 0.0 reduce-scatter.9.cloned.1.call-start
  11.6 0.7 compare_select_fusion
  12.3 235.6 %all-gather.3.cloned.1.call-done = bf16[768,4096]{0,1:T(8,128)(2,1)} async-done(((bf16[768,128]{0,1:T(8,128)(2,1)}), bf16[768,4096]{0,1:T(8,128)(2,1)}) %all-gather.3.cloned.1.call-update) | async-done | bytes 6291472 | tf_op jit(solution)/shard_map/all_gather | solution.py:25
  247.9 8.6 %copy.22 = bf16[768,32,128]{2,0,1:T(8,128)(2,1)} copy(bf16[768,32,128]{0,2,1:T(8,128)(2,1)} %bitcast.72) | data formatting | bytes 12582912 | tf_op jit(solution)/shard_map/reshape | solution.py:26
  256.5 225.1 %all-gather.5.cloned.1.call-done = bf16[768,4096]{0,1:T(8,128)(2,1)} async-done(((bf16[768,128]{0,1:T(8,128)(2,1)}), bf16[768,4096]{0,1:T(8,128)(2,1)}) %all-gather.5.cloned.1.call-update) | async-done | bytes 6291472 | tf_op jit(solution)/shard_map/all_gather | solution.py:33
  481.6 8.6 %copy.24 = bf16[768,32,128]{2,0,1:T(8,128)(2,1)} copy(bf16[768,32,128]{0,2,1:T(8,128)(2,1)} %bitcast.74) | data formatting | bytes 12582912 | tf_op jit(solution)/shard_map/reshape | solution.py:34
  490.2 6.8 gather_fusion
  496.9 6.8 gather_fusion.1
  503.7 0.0 copy-done
  503.7 0.0 copy-start.1
  503.7 4.9 bitcast_reduce_fusion
  508.7 0.0 copy-start.3
  508.7 0.0 copy-done.1
  508.7 2.9 fusion.30
  511.5 0.0 copy-done.3
  511.6 1.0 copy.34
  512.5 0.0 copy-start.2
  512.6 1.4 copy.45
  514.0 0.0 reduce-scatter.9.cloned.1.call-update
  514.0 0.2 reduce-scatter.7.cloned.1.call-start
  514.2 0.0 copy-done.2
  514.2 0.0 copy-start.4
  514.3 4.9 bitcast_reduce_fusion.1
  519.2 0.0 copy-done.4
  519.2 6.5 fusion.27
  525.7 0.7 copy.32
  526.4 1.4 copy.46
  527.8 0.0 reduce-scatter.7.cloned.1.call-update
  527.8 92.1 %reduce-scatter.9.cloned.1.call-done = bf16[8,4096]{1,0:T(8,128)(2,1)} async-done(((bf16[128,4096]{1,0:T(8,128)(2,1)}), bf16[8,4096]{1,0:T(8,128)(2,1)}) %reduce-scatter.9.cloned.1.call-update) | async-done | bytes 65552
  619.9 0.8 copy.47
  620.7 0.7 copy.35
  621.4 102.0 %reduce-scatter.7.cloned.1.call-done = bf16[8,4096]{1,0:T(8,128)(2,1)} async-done(((bf16[128,4096]{1,0:T(8,128)(2,1)}), bf16[8,4096]{1,0:T(8,128)(2,1)}) %reduce-scatter.7.cloned.1.call-update) | async-done | bytes 65552
  723.4 0.8 copy.48
  724.3 0.7 copy.33
  (2 shorter events, 0.0 us)
Async XLA Ops:
  7.2 496.6 %copy-start = (bf16[32,128,128]{2,1,0:T(8,128)(2,1)S(1)}, bf16[32,128,128]{2,1,0:T(8,128)(2,1)}, u32[]{:S(2)}) copy-start(bf16[32,128,128]{2,1,0:T(8,128)(2,1)} %param.8) | copy-start | bytes 3145732
  7.2 240.7 %all-gather.3.cloned.1.call-start = ((), (), s32[]{:S(2)}) async-start(), calls=%async_computation.2 | async-start | bytes 6488064 | tf_op jit(solution)/shard_map/all_gather | solution.py:25
  9.1 472.5 %all-gather.5.cloned.1.call-start = ((), (), s32[]{:S(2)}) async-start(), calls=%async_computation.3 | async-start | bytes 6488064 | tf_op jit(solution)/shard_map/all_gather | solution.py:33
  11.6 608.3 %reduce-scatter.9.cloned.1.call-start = ((), (), s32[]{:S(2)}) async-start(), calls=%async_computation.5 | async-start | bytes 1114112
  503.7 4.9 copy-start.1
  508.7 2.9 copy-start.3
  512.5 1.7 copy-start.2
  514.0 209.4 %reduce-scatter.7.cloned.1.call-start = ((), (), s32[]{:S(2)}) async-start(), calls=%async_computation.4 | async-start | bytes 1114112
  514.2 5.0 copy-start.4
Sparse Core Ops, SparseCore 0:
  10.1 237.7 all-gather.2
  250.0 231.5 all-gather.4
  514.1 105.7 reduce-scatter.8
  625.1 98.2 reduce-scatter.6
where the time goes:
time: 732 us; the launch traced here: 731 us
  waiting for transfers between devices  655 us (89%)
  local copies, waits for them, and re-layouts  41.2 us (6%)
  matrix products  19.2 us (3%)
  between operations  14.5 us (2%)
    all_gather x1, waiting for transfers between devices, shards(): features = lax.all_gather(tokens, 'blk', axis=1, tiled=True)  236 us
    all_gather x1, waiting for transfers between devices, shards(): gradient = lax.all_gather(masked, 'blk', axis=1, tiled=True)  225 us
    unnamed x6, waiting for transfers between devices  194 us
  transfers between devices with their start and end apart: 4, of which 4 were waited for; matrix products, arithmetic and copies ran while one was open for 4% of the time, Pallas kernels for 0%

commit v1 on v0

--- a/solution.py
+++ b/solution.py
@@ -22,7 +22,10 @@
     groups = input_weight_blocks.shape[0] // BLOCKS_PER_COLUMN
     live_rows = lax.iota(jnp.int32, tok_rows)[:, None] < lengths[0]
     masked = jnp.where(live_rows, grad_out, jnp.zeros_like(grad_out))
-    features = lax.all_gather(tokens, "blk", axis=1, tiled=True)
+    n_dev = lax.axis_size("blk")
+    blocks = jnp.stack([tokens for _ in range(n_dev)])
+    blocks = lax.all_to_all(blocks, "blk", split_axis=0, concat_axis=0)
+    features = jnp.concatenate(blocks, axis=1)
     x_slots = features.reshape(tok_rows, -1, BLOCK_SIDE)[:, row_ids, :]
     pre_slot = jnp.einsum(
         "tkc,kch->tkh", x_slots, input_weight_blocks, preferred_element_type=jnp.float32

time: 732 us -> 638 us (0.87)
  waiting for transfers between devices: 655 us -> 548 us
  starting transfers between devices: 0.34 us -> 16.2 us
    all_gather x1 -> x0, waiting for transfers between devices: 236 us -> none  [shards(): features = lax.all_gather(tokens, 'blk', axis=1, tiled=True)]
    all_gather x1, waiting for transfers between devices: 225 us -> 316 us  [shards(): gradient = lax.all_gather(masked, 'blk', axis=1, tiled=True)]
    unnamed x6 -> x5, waiting for transfers between devices: 194 us -> 232 us
    all_to_all x0 -> x1, starting transfers between devices: none -> 15.9 us  [shards(): blocks = lax.all_to_all(blocks, 'blk', split_axis=0, concat_axis=0)]
    reshape x1 -> x0, local copies, waits for them, and re-layouts: 8.62 us -> none  [shards(): x_slots = features.reshape(tok_rows, -1, BLOCK_SIDE)[:, row_ids, :]]
  transfers between devices with their start and end apart: 4 -> 4, of which waited for: 4 -> 3; matrix products, arithmetic and copies ran while one was open for 4% -> 5% of each run, Pallas kernels for 0% -> 0%
where the time goes in v1:
time: 638 us; the launch traced here: 637 us
  waiting for transfers between devices  548 us (86%)
  local copies, waits for them, and re-layouts  35.6 us (6%)
  matrix products  21.7 us (3%)
  starting transfers between devices  16.2 us (3%)
  between operations  14.5 us (2%)
    all_gather x1, waiting for transfers between devices, shards(): gradient = lax.all_gather(masked, 'blk', axis=1, tiled=True)  316 us
    unnamed x5, waiting for transfers between devices  232 us
    all_to_all x1, starting transfers between devices, shards(): blocks = lax.all_to_all(blocks, 'blk', split_axis=0, concat_axis=0)  15.9 us
  transfers between devices with their start and end apart: 4, of which 3 were waited for; matrix products, arithmetic and copies ran while one was open for 5% of the time, Pallas kernels for 0%

profile of v1, /device:TPU:8, one launch (start us, length us, event | category | flops | bytes accessed | tf_op | source)
XLA Modules:
  0.0 637.2 jit_solution(9291599465245371389)
XLA Ops:
  7.2 0.0 copy-start
  7.2 5.0 stack.2
  12.2 0.0 copy-start.2
  12.2 0.0 copy-start.4
  12.2 15.9 %all-to-all-start = ((bf16[32,768,128]{2,1,0:T(8,128)(2,1)}), bf16[32,768,128]{2,1,0:T(8,128)(2,1)}, u32[]{:S(2)}, u32[]{:S(2)}) async-start(bf16[32,768,128]{2,1,0:T(8,128)(2,1)} %stack.2), calls=%async_computation | async-start | bytes 12582912 | tf_op jit(solution)/shard_map/all_to_all | solution.py:27
  28.2 0.0 all-gather.2.cloned.1.call-start
  28.2 0.0 copy-done.2
  28.2 0.1 copy.20
  29.0 0.7 broadcast_select_fusion
  29.7 0.0 all-gather.2.cloned.1.call-update
  29.8 0.0 reduce-scatter.7.cloned.1.call-start
  29.8 0.0 copy-done.4
  29.8 316.5 %all-gather.2.cloned.1.call-done = bf16[768,4096]{0,1:T(8,128)(2,1)} async-done(((bf16[768,128]{0,1:T(8,128)(2,1)}), bf16[768,4096]{0,1:T(8,128)(2,1)}) %all-gather.2.cloned.1.call-update) | async-done | bytes 6291472 | tf_op jit(solution)/shard_map/all_gather | solution.py:36
  346.3 8.7 %copy.21 = bf16[768,32,128]{2,0,1:T(8,128)(2,1)} copy(bf16[768,32,128]{0,2,1:T(8,128)(2,1)} %bitcast.74) | data formatting | bytes 12582912 | tf_op jit(solution)/shard_map/reshape | solution.py:37
  355.0 6.8 %gather_fusion.1 = bf16[32,768,128]{2,1,0:T(8,128)(2,1)} fusion(bf16[768,32,128]{2,0,1:T(8,128)(2,1)} %copy.21, s32[1024]{0:T(1024)S(1)} %pad_clamp_fusion), kind=kCustom, calls=%fused_computation.1 | custom fusion | bytes 12583040 | tf_op jit(solution)/shard_map/gather | solution.py:37
  361.8 0.0 copy-done
  361.8 6.4 %bitcast_reduce_fusion.1 = f32[768,8,128]{2,0,1:T(8,128)} fusion(bf16[32,128,128]{2,1,0:T(8,128)(2,1)S(1)} %copy-done, bf16[32,768,128]{2,1,0:T(8,128)(2,1)} %gather_fusion.1), kind=kOutput, calls=%fused_computation.3 | convolution fusion | flops 807665664 | bytes 10485760 | tf_op jit(solution)/shard_map/xcn,cpn->xcp/dot_general | solution.py:43
  368.2 0.0 all-to-all-done
  368.2 0.0 copy-start.3
  368.2 6.8 %gather_fusion = bf16[32,768,128]{2,1,0:T(8,128)(2,1)} fusion(bf16[768,32,128]{2,0,1:T(8,128)(2,1)} %bitcast, s32[1024]{0:T(1024)S(1)} %pad_clamp_fusion), kind=kCustom, calls=%fused_computation | custom fusion | bytes 12583040 | tf_op jit(solution)/shard_map/gather | solution.py:29
  375.1 0.0 copy-done.3
  375.1 0.0 copy-start.1
  375.1 0.0 copy-start.6
  375.1 4.9 bitcast_reduce_fusion
  380.0 0.0 copy-start.5
  380.0 0.0 copy-done.1
  380.0 0.5 copy-done.6
  380.6 3.9 fusion.27
  384.5 0.0 copy-done.5
  384.5 0.7 copy.27
  385.2 1.4 copy.41
  386.6 0.0 reduce-scatter.7.cloned.1.call-update
  386.7 0.2 reduce-scatter.9.cloned.1.call-start
  386.9 6.5 %fusion.30 = bf16[8,4,128,128]{3,2,1,0:T(8,128)(2,1)S(1)} fusion(bf16[768,8,4,128]{3,0,2,1:T(8,128)(2,1)} %bitcast.73, f32[768,8,128]{2,0,1:T(8,128)} %copy-done.5), kind=kOutput, calls=%fused_computation.30 | convolution fusion | flops 812908544 | bytes 10485760 | tf_op jit(solution)/shard_map/tgh,tgrf->grhf/dot_general | solution.py:39
  393.3 1.0 copy.29
  394.3 1.4 copy.40
  395.7 0.0 reduce-scatter.9.cloned.1.call-update
  395.8 129.7 %reduce-scatter.7.cloned.1.call-done = bf16[8,4096]{1,0:T(8,128)(2,1)} async-done(((bf16[128,4096]{1,0:T(8,128)(2,1)}), bf16[8,4096]{1,0:T(8,128)(2,1)}) %reduce-scatter.7.cloned.1.call-update) | async-done | bytes 65552
  525.5 0.8 copy.43
  526.3 0.7 copy.28
  527.0 102.2 %reduce-scatter.9.cloned.1.call-done = bf16[8,4096]{1,0:T(8,128)(2,1)} async-done(((bf16[128,4096]{1,0:T(8,128)(2,1)}), bf16[8,4096]{1,0:T(8,128)(2,1)}) %reduce-scatter.9.cloned.1.call-update) | async-done | bytes 65552
  629.2 0.8 copy.42
  630.1 0.7 copy.30
  (3 shorter events, 0.0 us)
Async XLA Ops:
  7.2 354.6 %copy-start = (bf16[32,128,128]{2,1,0:T(8,128)(2,1)S(1)}, bf16[32,128,128]{2,1,0:T(8,128)(2,1)}, u32[]{:S(2)}) copy-start(bf16[32,128,128]{2,1,0:T(8,128)(2,1)} %param.9) | copy-start | bytes 3145732
  12.2 16.0 %copy-start.2 = (bf16[768,128]{1,0:T(8,128)(2,1)S(1)}, bf16[768,128]{1,0:T(8,128)(2,1)}, u32[]{:S(2)}) copy-start(bf16[768,128]{1,0:T(8,128)(2,1)} %param.7) | copy-start | bytes 589828
  12.2 17.6 %copy-start.4 = (s32[32]{0:T(128)S(1)}, s32[32]{0:T(128)}, u32[]{:S(2)}) copy-start(s32[32]{0:T(128)} %param.10) | copy-start | bytes 388
  12.2 356.0 %all-to-all-start = ((bf16[32,768,128]{2,1,0:T(8,128)(2,1)}), bf16[32,768,128]{2,1,0:T(8,128)(2,1)}, u32[]{:S(2)}, u32[]{:S(2)}) async-start(bf16[32,768,128]{2,1,0:T(8,128)(2,1)} %stack.2), calls=%async_computation | async-start | bytes 12582912 | tf_op jit(solution)/shard_map/all_to_all | solution.py:27
  28.2 318.2 %all-gather.2.cloned.1.call-start = ((), (), s32[]{:S(2)}) async-start(), calls=%async_computation.3 | async-start | bytes 6488064 | tf_op jit(solution)/shard_map/all_gather | solution.py:36
  29.8 495.7 %reduce-scatter.7.cloned.1.call-start = ((), (), s32[]{:S(2)}) async-start(), calls=%async_computation.4 | async-start | bytes 1114112
  368.2 6.8 %copy-start.3 = (bf16[32,128,128]{2,1,0:T(8,128)(2,1)S(1)}, bf16[32,128,128]{2,1,0:T(8,128)(2,1)}, u32[]{:S(2)}) copy-start(bf16[32,128,128]{2,1,0:T(8,128)(2,1)} %param.8) | copy-start | bytes 3145732
  375.1 5.0 copy-start.1
  375.1 5.5 copy-start.6
  380.0 4.5 copy-start.5
  386.7 242.5 %reduce-scatter.9.cloned.1.call-start = ((), (), s32[]{:S(2)}) async-start(), calls=%async_computation.5 | async-start | bytes 1114112
Sparse Core Ops, SparseCore 0:
  31.1 315.1 all-gather.1
  386.8 138.6 reduce-scatter.6
  530.9 98.2 reduce-scatter.8
